TPU v7x, 256 devices: a whole 4x4x8 slice. The times are simulated.
256 devices in a mesh: gx: 4 (over x_lo, core), gy: 16 (over x_hi, z), gz: 4 (over y).
Axes of the slice: x: 4 (x_hi: 2, x_lo: 2; x = x_hi * 2 + x_lo), y: 4, z: 8, core: 2. Of those that a mesh axis runs over, the one named last changes fastest.
Arguments:
- field: bfloat16 [64, 8, 384, 1536], P(None, 'gz', 'gy', 'gx'), may hold values from -200 to 200, as said below
- mode_one_factor: bfloat16 [1536, 256], P('gx'), may hold values from -0.15625 to 0.15625
- mode_two_factor: bfloat16 [384, 256], P('gy'), may hold values from -0.3125 to 0.3125
Outputs:
- gram_one: float32 [1536, 1536], P('gx')
- gram_two: float32 [384, 384], P('gy')
- core: bfloat16 [64, 8, 256, 256], P('gx', 'gz', 'gy')
Inputs may be any that keep to these rules, and one draw needn't show every extreme that they name: `field`: the snapshot's values lie within -200 and 200.
All inputs are finite; a program needn't handle non-finite values.
Results may differ from a plain program's by a relative error of at most 0.005.
Values may be sent and summed in bfloat16 or wider, within the bound.
A program may use at most 128 MiB of HBM per device.

v0:
```python
import jax
import jax.numpy as jnp
from jax import lax
from jax.sharding import PartitionSpec as P


def local(field, mode_one_factor, mode_two_factor):
    vars_all, cells_three, cells_two, cells_one = field.shape
    rank_one = mode_one_factor.shape[1]
    count_gx = lax.axis_size("gx")
    own_rows = vars_all // count_gx
    total_three = cells_three * lax.axis_size("gz")
    total_two = cells_two * lax.axis_size("gy")
    flat_own = field.reshape(-1, cells_one)
    piece = lax.all_gather(field, "gx", axis=3, tiled=True)
    width = piece.shape[3]
    gram_block = lax.dot_general(
        flat_own,
        piece.reshape(-1, width),
        (((0,), (0,)), ((), ())),
        preferred_element_type=jnp.float32,
    )
    product = jnp.dot(
        field.reshape(-1, cells_one), mode_one_factor, preferred_element_type=jnp.float32
    )
    shrunk_sum = lax.psum_scatter(
        product.reshape(own_rows * lax.axis_size("gx"), cells_three, cells_two, rank_one),
        "gx",
        scatter_dimension=0,
        tiled=True,
    )
    gram_one = lax.psum(gram_block, ("gy", "gz")) * (1.0 / (vars_all * total_three * total_two))
    shrunk = shrunk_sum.astype(jnp.bfloat16)
    gram_two_block = jnp.einsum(
        "akjr,akqr->jq",
        shrunk,
        lax.all_gather(shrunk, "gy", axis=2, tiled=True),
        preferred_element_type=jnp.float32,
    )
    partial_core = jnp.einsum(
        "akjr,js->aksr", shrunk, mode_two_factor, preferred_element_type=jnp.float32
    )
    core = lax.psum_scatter(partial_core, "gy", scatter_dimension=2, tiled=True).astype(
        jnp.bfloat16
    )
    gram_two = lax.psum(gram_two_block, ("gx", "gz")) * (1.0 / (vars_all * total_three * rank_one))
    return (gram_one, gram_two, core)


def solution(mesh):
    placed = (P(None, "gz", "gy", "gx"), P("gx", None), P("gy", None))
    return jax.shard_map(
        local,
        mesh=mesh,
        in_specs=placed,
        out_specs=(P("gx", None), P("gy", None), P("gx", "gz", "gy", None)),
        check_vma=False,
    )
```

profile of v0, /device:TPU:8, one launch (start us, length us, event | category | flops | bytes accessed | tf_op | source)
XLA Modules:
  0.0 1197.3 jit_solution(16504379202459117194)
XLA Ops:
  7.2 0.0 copy-start
  7.2 0.0 all-gather.3.cloned.1.call-start
  7.2 3.7 copy.9
  10.9 0.0 all-gather.3.cloned.1.call-update
  10.9 0.0 reduce-scatter.3.cloned.1.call-start
  11.0 0.0 copy-done
  11.0 1.6 copy-done.1
  12.6 2.6 fusion.5
  15.2 0.0 reduce-scatter.3.cloned.1.call-update
  15.2 0.0 all-reduce.2.cloned.1.call-start
  15.3 89.8 %all-gather.3.cloned.1.call-done = bf16[64,2,24,1536]{3,0,2,1:T(8,128)(2,1)} async-done(((bf16[64,2,24,384]{3,0,2,1:T(8,128)(2,1)}), bf16[64,2,24,1536]{3,0,2,1:T(8,128)(2,1)}) %all-gather.3.cloned.1.call-update) | async-done | bytes 9437200 | tf_op jit(solution)/shard_map/all_gather | solution.py:15
  105.1 17.4 %fusion.2 = f32[384,1536]{1,0:T(8,128)} fusion(bf16[64,2,24,384]{3,2,1,0:T(8,128)(2,1)S(1)} %copy-done.1, bf16[64,2,24,1536]{3,0,2,1:T(8,128)(2,1)} %all-gather.3.cloned.1.call-done), kind=kOutput, calls=%fused_computation.3 | convolution fusion | flops 3623878656 | bytes 14155776 | tf_op jit(solution)/shard_map/dot_general | solution.py:17
  122.5 0.0 all-reduce.2.cloned.1.call-update
  122.5 0.0 all-gather.5.cloned.1.call-start
  122.5 26.8 %reduce-scatter.3.cloned.1.call-done = f32[16,2,24,256]{3,2,1,0:T(8,128)} async-done(((f32[64,2,24,256]{3,2,1,0:T(8,128)}), f32[16,2,24,256]{3,2,1,0:T(8,128)}) %reduce-scatter.3.cloned.1.call-update) | async-done | bytes 786448 | tf_op jit(solution)/shard_map/reduce_scatter | solution.py:26
  149.3 2.0 convert_element_type.6
  151.3 0.0 all-gather.5.cloned.1.call-update
  151.3 0.0 reduce-scatter.5.cloned.1.call-start
  151.3 0.0 copy-done.3
  151.4 5.5 convolution_bitcast_fusion
  156.9 10.5 copy.11
  167.4 0.0 reduce-scatter.5.cloned.1.call-update
  167.4 0.0 copy-start.2
  167.4 677.4 %all-reduce.2.cloned.1.call-done = f32[384,1536]{1,0:T(8,128)} async-done(((f32[384,1536]{1,0:T(8,128)}), f32[384,1536]{1,0:T(8,128)}) %all-reduce.2.cloned.1.call-update) | async-done | bytes 2359312 | tf_op jit(solution)/shard_map/psum | solution.py:32
  844.8 3.3 broadcast_multiply_fusion
  848.1 114.3 %all-gather.5.cloned.1.call-done = bf16[16,2,384,256]{3,2,1,0:T(8,128)(2,1)} async-done(((bf16[16,2,24,256]{3,2,1,0:T(8,128)(2,1)}), bf16[16,2,384,256]{3,2,1,0:T(8,128)(2,1)}) %all-gather.5.cloned.1.call-update) | async-done | bytes 6291472 | tf_op jit(solution)/shard_map/all_gather | solution.py:37
  962.4 4.5 convolution_bitcast_fusion.1
  966.9 52.5 %psum.15 = f32[24,384]{1,0:T(8,128)S(1)} all-reduce(f32[24,384]{1,0:T(8,128)S(1)} %convolution_bitcast_fusion.1), channel_id=1, replica_groups=mesh['gx'=4,'gy'=16,'gz'=4] {'gx','gz'}, use_global_device_ids=true, to_apply=%region_2.0 | all-reduce | flops 9216 | bytes 73728 | tf_op jit(solution)/shard_map/psum | solution.py:46
  1019.4 0.6 broadcast_multiply_fusion.1
  1020.0 168.8 %reduce-scatter.5.cloned.1.call-done = f32[16,2,16,256]{3,0,1,2:T(8,128)} async-done(((f32[16,2,256,256]{3,0,1,2:T(8,128)}), f32[16,2,16,256]{3,0,1,2:T(8,128)}) %reduce-scatter.5.cloned.1.call-update) | async-done | bytes 524304 | tf_op jit(solution)/shard_map/reduce_scatter | solution.py:43
  1188.8 1.1 convert_element_type.7
  1189.9 0.9 copy.12
  (3 shorter events, 0.0 us)
Async XLA Ops:
  7.2 3.8 copy-start
  7.2 97.9 %all-gather.3.cloned.1.call-start = ((), (), s32[]{:S(2)}) async-start(), calls=%async_computation.2 | async-start | bytes 11796480 | tf_op jit(solution)/shard_map/all_gather | solution.py:15
  10.9 1.7 copy-start.1
  10.9 138.4 %reduce-scatter.3.cloned.1.call-start = ((), (), s32[]{:S(2)}) async-start(), calls=%async_computation.4 | async-start | bytes 3932160 | tf_op jit(solution)/shard_map/reduce_scatter | solution.py:26
  15.2 829.6 %all-reduce.2.cloned.1.call-start = ((), (), s32[]{:S(2)}) async-start(), calls=%async_computation.3 | async-start | bytes 4718592 | tf_op jit(solution)/shard_map/psum | solution.py:32
  122.5 28.9 %copy-start.3 = (bf16[24,256]{1,0:T(8,128)(2,1)S(1)}, bf16[24,256]{1,0:T(8,128)(2,1)}, u32[]{:S(2)}) copy-start(bf16[24,256]{1,0:T(8,128)(2,1)} %param.5) | copy-start | bytes 36868
  122.5 839.9 %all-gather.5.cloned.1.call-start = ((), (), s32[]{:S(2)}) async-start(), calls=%async_computation.5 | async-start | bytes 6684672 | tf_op jit(solution)/shard_map/all_gather | solution.py:37
  151.3 1037.5 %reduce-scatter.5.cloned.1.call-start = ((), (), s32[]{:S(2)}) async-start(), calls=%async_computation.6 | async-start | bytes 8912896 | tf_op jit(solution)/shard_map/reduce_scatter | solution.py:43
  167.4 795.0 %copy-start.2 = (bf16[16,2,24,256]{3,2,1,0:T(8,128)(2,1)S(1)}, bf16[16,2,24,256]{3,2,1,0:T(8,128)(2,1)}, u32[]{:S(2)}) copy-start(bf16[16,2,24,256]{3,2,1,0:T(8,128)(2,1)} %convert_element_type.6) | copy-start | bytes 1179652
Sparse Core Ops, SparseCore 0:
  11.1 93.9 all-gather.2
  107.6 41.6 reduce-scatter.2
  152.5 692.2 all-reduce.1
  847.3 115.0 all-gather.4
  966.3 222.4 reduce-scatter.4
where the time goes:
time: 1200 us
  waiting for transfers between devices  1080 us (90%)
  blocking collectives  52.5 us (4%)
  matrix products  30.1 us (3%)
  local copies, waits for them, and re-layouts  16.6 us (1%)
  between operations  13.8 us (1%)
    psum x1, waiting for transfers between devices, local(): lax.psum(gram_block, ('gy', 'gz'))  677 us
    reduce_scatter x1, waiting for transfers between devices, local(): lax.psum_scatter(partial_core, 'gy', scatter_dimension=2, tiled=True)  169 us
    all_gather x1, waiting for transfers between devices, local(): lax.all_gather(shrunk, 'gy', axis=2, tiled=True)  114 us
    all_gather x1, waiting for transfers between devices, local(): piece = lax.all_gather(field, 'gx', axis=3, tiled=True)  89.8 us
    psum x1, blocking collectives, local(): lax.psum(gram_two_block, ('gx', 'gz'))  52.5 us
    reduce_scatter x1, waiting for transfers between devices, local(): lax.psum_scatter(product.reshape(own_rows * lax.axis_size('gx'), cells_th...  26.8 us
  transfers between devices with their start and end apart: 5, of which 5 were waited for; matrix products, arithmetic and copies ran while one was open for 4% of the time, Pallas kernels for 0%

commit v1 on v0

--- a/solution.py
+++ b/solution.py
@@ -2,6 +2,13 @@
 import jax.numpy as jnp
 from jax import lax
 from jax.sharding import PartitionSpec as P
+
+
+def gather_over(value, name, dim):
+    n_dev = lax.axis_size(name)
+    blocks = jnp.stack([value for _ in range(n_dev)])
+    blocks = lax.all_to_all(blocks, name, split_axis=0, concat_axis=0)
+    return jnp.concatenate(blocks, axis=dim)
 
 
 def local(field, mode_one_factor, mode_two_factor):
@@ -12,7 +19,7 @@
     total_three = cells_three * lax.axis_size("gz")
     total_two = cells_two * lax.axis_size("gy")
     flat_own = field.reshape(-1, cells_one)
-    piece = lax.all_gather(field, "gx", axis=3, tiled=True)
+    piece = gather_over(field, "gx", 3)
     width = piece.shape[3]
     gram_block = lax.dot_general(
         flat_own,

time: 1200 us -> 973 us (0.81)
  waiting for transfers between devices: 1080 us -> 818 us
  local copies, waits for them, and re-layouts: 16.6 us -> 50.2 us
    reduce_scatter x1, waiting for transfers between devices: 169 us -> 0.01 us  [local(): lax.psum_scatter(partial_core, 'gy', scatter_dimension=2, tiled=True)]
    all_to_all x0 -> x1, waiting for transfers between devices: none -> 127 us  [gather_over(): blocks = lax.all_to_all(blocks, name, split_axis=0, concat_axis=0)]
    all_gather x1, waiting for transfers between devices: 114 us -> 0.01 us  [local(): lax.all_gather(shrunk, 'gy', axis=2, tiled=True)]
    all_gather x1 -> x0, waiting for transfers between devices: 89.8 us -> none  [local(): piece = lax.all_gather(field, 'gx', axis=3, tiled=True)]
    reduce_scatter x1, waiting for transfers between devices: 26.8 us -> 0.02 us  [local(): lax.psum_scatter(product.reshape(own_rows * lax.axis_size('gx'), cells_th...]
    reshape x0 -> x1, local copies, waits for them, and re-layouts: none -> 23.7 us  [gather_over(): return jnp.concatenate(blocks, axis=dim)]
    psum x1, waiting for transfers between devices: 677 us -> 691 us  [local(): lax.psum(gram_block, ('gy', 'gz'))]
  transfers between devices with their start and end apart: 5 -> 5, of which waited for: 5 -> 2; matrix products, arithmetic and copies ran while one was open for 4% -> 7% of each run, Pallas kernels for 0% -> 0%
where the time goes in v1:
time: 973 us; the launch traced here: 972 us
  waiting for transfers between devices  818 us (84%)
  blocking collectives  55.5 us (6%)
  local copies, waits for them, and re-layouts  50.2 us (5%)
  matrix products  20.5 us (2%)
  between operations  15.3 us (2%)
    psum x1, waiting for transfers between devices, local(): lax.psum(gram_block, ('gy', 'gz'))  691 us
    all_to_all x1, waiting for transfers between devices, gather_over(): blocks = lax.all_to_all(blocks, name, split_axis=0, concat_axis=0)  127 us
    psum x1, blocking collectives, local(): lax.psum(gram_two_block, ('gx', 'gz'))  55.5 us
    reshape x1, local copies, waits for them, and re-layouts, gather_over(): return jnp.concatenate(blocks, axis=dim)  23.7 us
  transfers between devices with their start and end apart: 5, of which 2 were waited for; matrix products, arithmetic and copies ran while one was open for 7% of the time, Pallas kernels for 0%

profile of v1, /device:TPU:8, one launch (start us, length us, event | category | flops | bytes accessed | tf_op | source)
XLA Modules:
  0.0 972.4 jit_solution(16921907441099503279)
XLA Ops:
  8.0 0.0 copy-start
  8.0 6.2 stack.2
  14.2 5.9 all-to-all-start
  20.1 0.0 reduce-scatter.3.cloned.1.call-start
  20.2 0.0 copy-done
  20.2 0.0 copy-done.2
  20.2 2.6 fusion
  22.8 0.0 reduce-scatter.3.cloned.1.call-update
  22.9 0.0 all-reduce.2.cloned.1.call-start
  22.9 126.9 %all-to-all-done = bf16[4,64,2,24,384]{4,3,2,1,0:T(8,128)(2,1)} async-done(((bf16[4,64,2,24,384]{4,3,2,1,0:T(8,128)(2,1)}), bf16[4,64,2,24,384]{4,3,2,1,0:T(8,128)(2,1)}, u32[]{:S(2)}, u32[]{:S(2)}) %all-to-all-start) | async-done | bytes 9437216 | tf_op jit(solution)/shard_map/all_to_all | solution.py:10
  149.8 23.7 %copy.8 = bf16[64,2,24,4,384]{4,3,2,1,0:T(4,128)(2,1)} copy(bf16[64,2,24,4,384]{4,2,1,0,3:T(8,128)(2,1)} %bitcast.1) | data formatting | bytes 18874368 | tf_op jit(solution)/shard_map/reshape | solution.py:11
  173.5 9.0 copy.14
  182.4 7.8 fusion.3
  190.3 0.0 all-reduce.2.cloned.1.call-update
  190.3 0.0 all-gather.2.cloned.1.call-start
  190.3 0.0 reduce-scatter.3.cloned.1.call-done
  190.4 2.0 convert_element_type.6
  192.3 0.0 all-gather.2.cloned.1.call-update
  192.3 0.0 reduce-scatter.5.cloned.1.call-start
  192.4 0.0 copy-done.4
  192.4 5.5 convolution_bitcast_fusion
  197.9 10.5 %copy.9 = f32[16,2,256,256]{3,0,1,2:T(8,128)} copy(f32[16,2,256,256]{2,3,1,0:T(8,128)} %convolution_bitcast_fusion) | data formatting | bytes 16777216 | tf_op jit(solution)/shard_map/akjr,js->aksr/transpose | solution.py:47
  208.4 0.0 reduce-scatter.5.cloned.1.call-update
  208.4 0.0 copy-start.3
  208.4 691.0 %all-reduce.2.cloned.1.call-done = f32[384,1536]{1,0:T(8,128)} async-done(((f32[384,1536]{1,0:T(8,128)}), f32[384,1536]{1,0:T(8,128)}) %all-reduce.2.cloned.1.call-update) | async-done | bytes 2359312 | tf_op jit(solution)/shard_map/psum | solution.py:39
  899.4 3.3 broadcast_multiply_fusion
  902.7 4.5 convolution_bitcast_fusion.1
  907.2 55.5 %psum.15 = f32[24,384]{1,0:T(8,128)S(1)} all-reduce(f32[24,384]{1,0:T(8,128)S(1)} %convolution_bitcast_fusion.1), channel_id=1, replica_groups=mesh['gx'=4,'gy'=16,'gz'=4] {'gx','gz'}, use_global_device_ids=true, to_apply=%region_2.0 | all-reduce | flops 9216 | bytes 73728 | tf_op jit(solution)/shard_map/psum | solution.py:53
  962.7 0.6 broadcast_multiply_fusion.1
  963.4 1.1 convert_element_type.7
  964.4 0.9 copy.10
  965.3 0.0 copy-done.1
  (6 shorter events, 0.0 us)
Async XLA Ops:
  8.0 12.2 %copy-start = (bf16[384,256]{1,0:T(8,128)(2,1)S(1)}, bf16[384,256]{1,0:T(8,128)(2,1)}, u32[]{:S(2)}) copy-start(bf16[384,256]{1,0:T(8,128)(2,1)} %param.4) | copy-start | bytes 589828
  14.2 6.0 copy-start.2
  14.2 135.6 %all-to-all-start = ((bf16[4,64,2,24,384]{4,3,2,1,0:T(8,128)(2,1)}), bf16[4,64,2,24,384]{4,3,2,1,0:T(8,128)(2,1)}, u32[]{:S(2)}, u32[]{:S(2)}) async-start(bf16[4,64,2,24,384]{4,3,2,1,0:T(8,128)(2,1)} %stack.2), calls=%async_computation | async-start | bytes 18874368 | tf_op jit(solution)/shard_map/all_to_all | solution.py:10
  20.1 170.2 %reduce-scatter.3.cloned.1.call-start = ((), (), s32[]{:S(2)}) async-start(), calls=%async_computation.4 | async-start | bytes 3932160 | tf_op jit(solution)/shard_map/reduce_scatter | solution.py:33
  22.9 876.5 %all-reduce.2.cloned.1.call-start = ((), (), s32[]{:S(2)}) async-start(), calls=%async_computation.3 | async-start | bytes 4718592 | tf_op jit(solution)/shard_map/psum | solution.py:39
  190.3 2.1 copy-start.4
  190.3 712.4 %all-gather.2.cloned.1.call-start = ((), (), s32[]{:S(2)}) async-start(), calls=%async_computation.5 | async-start | bytes 6684672 | tf_op jit(solution)/shard_map/all_gather | solution.py:44
  192.3 771.0 %reduce-scatter.5.cloned.1.call-start = ((), (), s32[]{:S(2)}) async-start(), calls=%async_computation.6 | async-start | bytes 8912896 | tf_op jit(solution)/shard_map/reduce_scatter | solution.py:50
  208.4 694.3 %copy-start.3 = (bf16[16,2,24,256]{3,2,1,0:T(8,128)(2,1)S(1)}, bf16[16,2,24,256]{3,2,1,0:T(8,128)(2,1)}, u32[]{:S(2)}) copy-start(bf16[16,2,24,256]{3,2,1,0:T(8,128)(2,1)} %convert_element_type.6) | copy-start | bytes 1179652
  899.4 65.9 %copy-start.1 = (bf16[384,256]{1,0:T(8,128)(2,1)S(1)}, bf16[384,256]{1,0:T(8,128)(2,1)}, u32[]{:S(2)}) copy-start(bf16[384,256]{1,0:T(8,128)(2,1)} %param.4) | copy-start | bytes 589828
Sparse Core Ops, SparseCore 0:
  23.5 68.1 reduce-scatter.2
  193.7 119.0 all-gather.1
  316.9 222.9 reduce-scatter.4
Sparse Core Ops, SparseCore 1:
  190.4 709.0 all-reduce.1
